TPU v7x, 256 devices: a whole 4x4x8 slice. The times are simulated.
256 devices in a mesh: dp: 64 (over z, y, core), tp: 4 (over x).
Axes of the slice: x: 4, y: 4, z: 8, core: 2. Of those that a mesh axis runs over, the one named last changes fastest.
Arguments:
- attn_partial: bfloat16 [4, 4096, 7168], P('tp', 'dp'), may hold values from -3 to 3
- hidden_in: bfloat16 [4096, 7168], P('dp', 'tp'), may hold values from -6 to 6
- norm_gain: float32 [7168], replicated, may hold values from 0.5 to 1.5
- expert_ids: int32 [4096, 8], P('dp'), may hold values from 0 to 255, all different within a row; in each aligned block of 64 rows (0 to 63, 64 to 127, ...) at most 4 rows name the same one
- route_prob: bfloat16 [4096, 8], P('dp'), may hold values from 0.049804688 to 0.3984375
- w_gate: bfloat16 [64, 7168, 1024], P('dp', None, 'tp'), may hold values from -0.0625 to 0.0625
- w_up: bfloat16 [64, 7168, 1024], P('dp', None, 'tp'), may hold values from -0.0625 to 0.0625
- w_down: bfloat16 [64, 1024, 7168], P('dp', 'tp'), may hold values from -0.1875 to 0.1875
Outputs:
- layer_out: bfloat16 [4096, 7168], P('dp', 'tp')
- amax_input: float32 [64], P('dp')
- amax_hidden: float32 [64], P('dp')
Inputs may be any that keep to these rules, and one draw needn't show every extreme that they name: `expert_ids`: each token names 8 different experts; within each aligned block of 64 tokens no expert is named by more than 4 tokens.
All inputs are finite; a program needn't handle non-finite values.
Results may differ from a plain program's by a relative error of at most 0.0075.
Values may be sent and summed in bfloat16 or wider, within the bound.
A program may use at most 64 MiB of HBM per device.

v0:
```python
import jax
import jax.numpy as jnp
from jax import lax
from jax.sharding import PartitionSpec as P

EXPERT_SLOTS = 4
eps = 1e-06


def route_tables(expert_ids, route_prob, experts, capacity):
    matches = expert_ids[:, :, None] == jnp.arange(experts, dtype=jnp.int32)[None, None, :]
    onehot = jnp.sum(matches.astype(jnp.int32), axis=1)
    weight = jnp.sum(
        jnp.where(matches, route_prob[:, :, None].astype(jnp.float32), jnp.float32(0.0)), axis=1
    )
    before = jnp.cumsum(onehot, axis=0) - onehot
    placing = (onehot.T[:, None, :] == 1) & (
        before.T[:, None, :] == jnp.arange(capacity, dtype=jnp.int32)[None, :, None]
    )
    return (onehot, weight, placing)


def on_device(attn_partial, hidden_in, norm_gain, expert_ids, route_prob, w_gate, w_up, w_down):
    experts = lax.axis_size("dp")
    dp_index = lax.axis_index("dp")
    tp_index = lax.axis_index("tp")
    partial_value = attn_partial[0].astype(jnp.float32)
    token_count = partial_value.shape[0]
    columns = hidden_in.shape[1]
    start_col = tp_index * columns
    own_cols = lax.dynamic_slice_in_dim(partial_value, start_col, columns, 1) + hidden_in.astype(
        jnp.float32
    )
    summand = lax.dynamic_update_slice_in_dim(partial_value, own_cols, start_col, 1)
    residual = lax.psum(summand, "tp")
    mean_sq = jnp.mean(residual * residual, axis=1, keepdims=True)
    normed = (residual * lax.rsqrt(mean_sq + eps) * norm_gain).astype(jnp.bfloat16)
    residual_cols = lax.dynamic_slice_in_dim(residual, start_col, columns, 1)
    onehot, weight, placing = route_tables(expert_ids, route_prob, experts, EXPERT_SLOTS)
    selection_mask = placing.reshape(experts * EXPERT_SLOTS, token_count).astype(jnp.bfloat16)
    outgoing = jnp.dot(selection_mask, normed, preferred_element_type=jnp.float32).astype(
        jnp.bfloat16
    )
    piece_width = outgoing.shape[1]
    incoming = lax.all_to_all(
        outgoing.reshape(experts, EXPERT_SLOTS, piece_width),
        "dp",
        split_axis=0,
        concat_axis=0,
        tiled=True,
    )
    expert_slot_rows = incoming.reshape(experts * EXPERT_SLOTS, piece_width)
    gate_val = jnp.dot(expert_slot_rows, w_gate[0], preferred_element_type=jnp.float32)
    up_val = jnp.dot(expert_slot_rows, w_up[0], preferred_element_type=jnp.float32)
    hidden_act = (jax.nn.silu(gate_val) * up_val).astype(jnp.bfloat16)
    partial_out = jnp.dot(hidden_act, w_down[0], preferred_element_type=jnp.float32)
    combine_matrix = (placing.astype(jnp.float32) * weight.T[:, None, :]).reshape(
        experts * EXPERT_SLOTS, token_count
    )
    expert_cols = lax.psum_scatter(
        partial_out.astype(jnp.bfloat16), "tp", scatter_dimension=1, tiled=True
    ).astype(jnp.float32)
    returned = lax.all_to_all(
        expert_cols.reshape(experts, EXPERT_SLOTS, columns).astype(jnp.bfloat16),
        "dp",
        split_axis=0,
        concat_axis=0,
        tiled=True,
    ).astype(jnp.float32)
    moe_out = jnp.dot(
        combine_matrix.T,
        returned.reshape(experts * EXPERT_SLOTS, columns),
        precision=lax.Precision.HIGHEST,
        preferred_element_type=jnp.float32,
    )
    layer_out = (residual_cols + moe_out).astype(jnp.bfloat16)
    hidden_peak = jnp.max(jnp.abs(hidden_act.astype(jnp.float32)))
    row_peak = jnp.max(jnp.abs(normed.astype(jnp.float32)), axis=1)
    local_entry = jnp.max(onehot.astype(jnp.float32) * row_peak[:, None], axis=0)
    own_slot = jnp.arange(experts, dtype=jnp.int32) == dp_index
    hidden_local = jnp.where(own_slot, hidden_peak, jnp.float32(0.0))
    every_entry, every_hidden = lax.pmax((local_entry, hidden_local), ("dp", "tp"))
    amax_input = lax.dynamic_slice_in_dim(every_entry, dp_index, 1, 0)
    amax_hidden = lax.dynamic_slice_in_dim(every_hidden, dp_index, 1, 0)
    return (layer_out, amax_input, amax_hidden)


def solution(mesh):
    placed = (
        P("tp", "dp", None),
        P("dp", "tp"),
        P(),
        P("dp", None),
        P("dp", None),
        P("dp", None, "tp"),
        P("dp", None, "tp"),
        P("dp", "tp", None),
    )
    return jax.shard_map(
        on_device,
        mesh=mesh,
        in_specs=placed,
        out_specs=(P("dp", "tp"), P("dp"), P("dp")),
        check_vma=False,
    )
```

profile of v0, /device:TPU:1, one launch (start us, length us, event | category | flops | bytes accessed | tf_op | source)
XLA Modules:
  0.0 342.8 jit_solution(10754556767076830818)
XLA Ops:
  7.2 0.0 copy-start.4
  7.2 0.0 all-reduce.3.cloned.1.call-start
  7.2 0.0 copy-start.6
  7.2 2.8 fusion.21
  10.1 0.0 copy-done.4
  10.1 1.1 fusion.14
  11.2 0.0 copy-start.1
  11.2 1.2 copy-done.1
  12.4 0.0 all-reduce.3.cloned.1.call-update
  12.4 0.0 reduce-scatter.2.cloned.1.call-start
  12.5 0.0 copy-done.6
  12.5 0.1 copy.26
  12.6 0.2 convert_reduce_fusion
  12.7 0.1 reduce_window_sum.11
  12.8 0.1 copy.28
  12.9 0.1 copy.27
  13.1 0.1 eq.64
  13.2 62.8 %all-reduce.3.cloned.1.call-done = f32[64,7168]{1,0:T(8,128)} async-done(((f32[64,7168]{1,0:T(8,128)}), f32[64,7168]{1,0:T(8,128)}) %all-reduce.3.cloned.1.call-update) | async-done | bytes 1835024 | tf_op jit(solution)/shard_map/psum | solution.py:35
  75.9 1.7 multiply_reduce_fusion
  77.7 0.0 copy-done.5
  77.7 4.5 %convolution_convert_fusion.1 = bf16[256,7168]{1,0:T(8,128)(2,1)} fusion(pred[256,64]{1,0:T(8,128)(4,1)S(1)} %bitcast.38, s32[256,64]{1,0:T(8,128)S(1)} %bitcast.37, s32[256]{0:T(256)S(1)} %eq.64, f32[64,7168]{1,0:T(8,128)} %all-reduce.3.cloned.1.call-done, f32[7168]{0:T(1024)S(1)} %copy-done.5, f32[64]{0:T(128)S(1)} %add_rsqrt_fusion), kind=kOutput, calls=%fused_computation.1 | convolution fusion | flops 238125056 | bytes 5616896 | tf_op jit(solution)/shard_map/dot_general | solution.py:41
  82.3 7.0 %reshape.39 = bf16[64,4,7168]{2,1,0:T(4,128)(2,1)} reshape(bf16[256,7168]{1,0:T(8,128)(2,1)} %convolution_convert_fusion.1) | data formatting | bytes 7340032 | tf_op jit(solution)/shard_map/reshape | solution.py:46
  89.3 94.8 %all_to_all.10 = bf16[64,4,7168]{2,1,0:T(4,128)(2,1)} all-to-all(bf16[64,4,7168]{2,1,0:T(4,128)(2,1)} %reshape.39), channel_id=1, replica_groups=mesh['dp'=64,'tp'=4] {'dp'}, dimensions={0} | all-to-all | bytes 7340032 | tf_op jit(solution)/shard_map/all_to_all | solution.py:45
  184.1 6.7 %reshape.40 = bf16[256,7168]{1,0:T(8,128)(2,1)} reshape(bf16[64,4,7168]{2,1,0:T(4,128)(2,1)} %all_to_all.10) | data formatting | bytes 7340032 | tf_op jit(solution)/shard_map/reshape | solution.py:52
  190.8 4.4 %fusion.3 = f32[256,256]{1,0:T(8,128)S(1)} fusion(bf16[256,7168]{1,0:T(8,128)(2,1)} %reshape.40, bf16[1,7168,256]{2,1,0:T(8,128)(2,1)} %param.13), kind=kOutput, calls=%fused_computation.5 | convolution fusion | flops 939524096 | bytes 7602176 | tf_op jit(solution)/shard_map/dot_general | solution.py:53
  195.2 0.0 copy-done.3
  195.2 0.9 copy-done.8
  196.1 1.7 abs_reduce_fusion.1
  197.9 0.3 copy-done.2
  198.2 2.9 convolution_convert_fusion
  201.1 0.0 reduce-scatter.2.cloned.1.call-update
  201.1 40.8 %reduce-scatter.2.cloned.1.call-done = bf16[256,1792]{1,0:T(8,128)(2,1)} async-done(((bf16[256,7168]{1,0:T(8,128)(2,1)}), bf16[256,1792]{1,0:T(8,128)(2,1)}) %reduce-scatter.2.cloned.1.call-update) | async-done | bytes 917520 | tf_op jit(solution)/shard_map/reduce_scatter | solution.py:60
  241.9 2.5 convert_element_type.57
  244.4 10.6 %all-to-all-start.1 = ((bf16[64,4,1792]{2,1,0:T(4,128)(2,1)}), bf16[64,4,1792]{2,1,0:T(4,128)(2,1)S(1)}, u32[]{:S(2)}, u32[]{:S(2)}) async-start(bf16[64,4,1792]{2,1,0:T(4,128)(2,1)} %convert_element_type.57), calls=%async_computation.2 | async-start | bytes 1835008 | tf_op jit(solution)/shard_map/all_to_all | solution.py:63
  255.1 0.0 copy-done.7
  255.1 0.1 copy.29
  255.2 0.2 select_reduce_fusion
  255.4 0.1 copy.30
  255.5 0.1 fusion.17
  255.5 0.0 copy-done
  255.5 0.4 abs_reduce_fusion
  255.9 0.1 multiply_reduce_fusion.1
  256.0 0.7 compare_select_fusion
  256.7 76.8 %all-reduce = (f32[64]{0:T(128)S(1)}, f32[64]{0:T(128)S(1)}) all-reduce(f32[64]{0:T(128)S(1)} %multiply_reduce_fusion.1, f32[64]{0:T(128)S(1)} %compare_select_fusion), channel_id=1, replica_groups=mesh['dp'=64,'tp'=4] {'dp','tp'}, use_global_device_ids=true, to_apply=%region_8.9 | all-reduce | flops 128 | bytes 1024 | tf_op jit(solution)/shard_map/pmax | solution.py:82
  333.5 0.6 dynamic_slice.18
  334.1 0.6 dynamic_slice.17
  334.7 0.0 all-to-all-done.1
  334.7 1.3 fusion.6
  (12 shorter events, 0.1 us)
Async XLA Ops:
  7.2 2.9 copy-start.4
  7.2 68.7 %all-reduce.3.cloned.1.call-start = ((), (), s32[]{:S(2)}) async-start(), calls=%async_computation.3 | async-start | bytes 3670016 | tf_op jit(solution)/shard_map/psum | solution.py:35
  7.2 5.3 %copy-start.6 = (s32[64,8]{0,1:T(8,128)S(1)}, s32[64,8]{0,1:T(8,128)}, u32[]{:S(2)}) copy-start(s32[64,8]{0,1:T(8,128)} %param.11) | copy-start | bytes 6148
  10.1 67.7 %copy-start.5 = (f32[7168]{0:T(1024)S(1)}, f32[7168]{0:T(1024)}, u32[]{:S(2)}) copy-start(f32[7168]{0:T(1024)} %param.10) | copy-start | bytes 86020
  11.2 1.3 copy-start.1
  12.4 229.5 %reduce-scatter.2.cloned.1.call-start = ((), (), s32[]{:S(2)}) async-start(), calls=%async_computation.4 | async-start | bytes 4587520 | tf_op jit(solution)/shard_map/reduce_scatter | solution.py:60
  190.8 4.4 %copy-start.3 = (bf16[256,7168]{1,0:T(8,128)(2,1)S(1)}, bf16[256,7168]{1,0:T(8,128)(2,1)}, u32[]{:S(2)}) copy-start(bf16[256,7168]{1,0:T(8,128)(2,1)} %reshape.40) | copy-start | bytes 11010052
  190.8 5.3 %copy-start.8 = (bf16[1,7168,256]{2,1,0:T(8,128)(2,1)S(1)}, bf16[1,7168,256]{2,1,0:T(8,128)(2,1)}, u32[]{:S(2)}) copy-start(bf16[1,7168,256]{2,1,0:T(8,128)(2,1)} %param.14) | copy-start | bytes 11010052
  196.1 2.0 copy-start.2
  201.1 54.0 %copy-start.7 = (bf16[64,8]{0,1:T(8,128)(2,1)S(1)}, bf16[64,8]{0,1:T(8,128)(2,1)}, u32[]{:S(2)}) copy-start(bf16[64,8]{0,1:T(8,128)(2,1)} %param.12) | copy-start | bytes 3076
  201.1 54.4 %copy-start = (f32[64,7168]{1,0:T(8,128)S(1)}, f32[64,7168]{1,0:T(8,128)}, u32[]{:S(2)}) copy-start(f32[64,7168]{1,0:T(8,128)} %all-reduce.3.cloned.1.call-done) | copy-start | bytes 5505028
  244.4 90.2 %all-to-all-start.1 = ((bf16[64,4,1792]{2,1,0:T(4,128)(2,1)}), bf16[64,4,1792]{2,1,0:T(4,128)(2,1)S(1)}, u32[]{:S(2)}, u32[]{:S(2)}) async-start(bf16[64,4,1792]{2,1,0:T(4,128)(2,1)} %convert_element_type.57), calls=%async_computation.2 | async-start | bytes 1835008 | tf_op jit(solution)/shard_map/all_to_all | solution.py:63
Sparse Core Ops, SparseCore 0:
  12.6 63.3 all-reduce.2
  201.2 40.6 reduce-scatter.1
where the time goes:
time: 344 us; the launch traced here: 343 us
  blocking collectives  172 us (50%)
  waiting for transfers between devices  104 us (30%)
  local copies, waits for them, and re-layouts  20.5 us (6%)
  matrix products  14.9 us (4%)
  between operations  14.2 us (4%)
  starting transfers between devices  10.7 us (3%)
  other arithmetic  7.3 us (2%)
    all_to_all x1, blocking collectives, on_device(): lax.all_to_all(outgoing.reshape(experts, EXPERT_SLOTS, piece_width), 'dp'...  94.8 us
    pmax x1, blocking collectives, on_device(): lax.pmax((local_entry, hidden_local), ('dp', 'tp'))  76.8 us
    psum x1, waiting for transfers between devices, on_device(): residual = lax.psum(summand, 'tp')  62.8 us
    reduce_scatter x1, waiting for transfers between devices, on_device(): lax.psum_scatter(partial_out.astype(jnp.bfloat16), 'tp', scatter_dimensio...  40.8 us
    all_to_all x1, starting transfers between devices, on_device(): lax.all_to_all(expert_cols.reshape(experts, EXPERT_SLOTS, columns).astype...  10.6 us
    reshape x1, local copies, waits for them, and re-layouts, on_device(): outgoing.reshape(experts, EXPERT_SLOTS, piece_width)  7 us
  transfers between devices with their start and end apart: 3, of which 2 were waited for; matrix products, arithmetic and copies ran while one was open for 1% of the time, Pallas kernels for 0%

commit v1 on v0

--- a/solution.py
+++ b/solution.py
@@ -32,7 +32,9 @@
         jnp.float32
     )
     summand = lax.dynamic_update_slice_in_dim(partial_value, own_cols, start_col, 1)
-    residual = lax.psum(summand, "tp")
+    residual = summand
+    for hop in (1, 2):
+        residual = residual + lax.ppermute(residual, "tp", [(dev, dev ^ hop) for dev in range(4)])
     mean_sq = jnp.mean(residual * residual, axis=1, keepdims=True)
     normed = (residual * lax.rsqrt(mean_sq + eps) * norm_gain).astype(jnp.bfloat16)
     residual_cols = lax.dynamic_slice_in_dim(residual, start_col, columns, 1)

time: 344 us -> 368 us (1.070)
  waiting for transfers between devices: 104 us -> 119 us
  starting transfers between devices: 10.7 us -> 16.8 us
    ppermute x0 -> x2, waiting for transfers between devices: none -> 76.5 us  [on_device(): lax.ppermute(residual, 'tp', [(dev, dev ^ hop) for dev in range(4)])]
    psum x1 -> x0, waiting for transfers between devices: 62.8 us -> none  [on_device(): residual = lax.psum(summand, 'tp')]
    ppermute x0 -> x2, starting transfers between devices: none -> 6.15 us  [on_device(): lax.ppermute(residual, 'tp', [(dev, dev ^ hop) for dev in range(4)])]
  transfers between devices with their start and end apart: 3 -> 4, of which waited for: 2 -> 3; matrix products, arithmetic and copies ran while one was open for 1% -> 1% of each run, Pallas kernels for 0% -> 0%
where the time goes in v1:
time: 368 us; the launch traced here: 367 us
  blocking collectives  175 us (48%)
  waiting for transfers between devices  119 us (32%)
  local copies, waits for them, and re-layouts  19.2 us (5%)
  starting transfers between devices  16.8 us (5%)
  between operations  14.2 us (4%)
  matrix products  13.4 us (4%)
  other arithmetic  9.39 us (3%)
    all_to_all x1, blocking collectives, on_device(): lax.all_to_all(outgoing.reshape(experts, EXPERT_SLOTS, piece_width), 'dp'...  98.5 us
    pmax x1, blocking collectives, on_device(): lax.pmax((local_entry, hidden_local), ('dp', 'tp'))  76.8 us
    ppermute x2, waiting for transfers between devices, on_device(): lax.ppermute(residual, 'tp', [(dev, dev ^ hop) for dev in range(4)])  76.5 us
    reduce_scatter x1, waiting for transfers between devices, on_device(): lax.psum_scatter(partial_out.astype(jnp.bfloat16), 'tp', scatter_dimensio...  42.3 us
    all_to_all x1, starting transfers between devices, on_device(): lax.all_to_all(expert_cols.reshape(experts, EXPERT_SLOTS, columns).astype...  10.6 us
  transfers between devices with their start and end apart: 4, of which 3 were waited for; matrix products, arithmetic and copies ran while one was open for 1% of the time, Pallas kernels for 0%

profile of v1, /device:TPU:1, one launch (start us, length us, event | category | flops | bytes accessed | tf_op | source)
XLA Modules:
  0.0 367.2 jit_solution(8077157244450657863)
XLA Ops:
  7.2 0.0 reduce-scatter.2.cloned.1.call-start
  7.2 0.0 copy-start.2
  7.2 2.8 fusion.23
  10.1 0.0 copy-done.2
  10.1 1.1 fusion.12
  11.1 0.0 copy-start.4
  11.1 2.1 collective-permute-start
  13.3 38.4 %collective-permute-done = f32[64,7168]{1,0:T(8,128)S(1)} collective-permute-done((f32[64,7168]{1,0:T(8,128)S(1)}, f32[64,7168]{1,0:T(8,128)S(1)}, u32[]{:S(2)}, u32[]{:S(2)}) %collective-permute-start) | collective-permute-done | bytes 1835040 | tf_op jit(solution)/shard_map/ppermute | solution.py:37
  51.7 1.5 add.40
  53.1 4.0 %collective-permute-start.1 = (f32[64,7168]{1,0:T(8,128)}, f32[64,7168]{1,0:T(8,128)}, u32[]{:S(2)}, u32[]{:S(2)}) collective-permute-start(f32[64,7168]{1,0:T(8,128)} %add.40), channel_id=1, source_target_pairs={{0,2},{1,3},{2,0},{3,1},{4,6},{5,7},{6,4},{7,5},{8,10},{9,11},{10,... | collective-permute-start | bytes 5505032 | tf_op jit(solution)/shard_map/ppermute | solution.py:37
  57.2 0.0 copy-done.4
  57.2 0.1 copy.26
  57.2 0.2 convert_reduce_fusion
  57.4 0.1 reduce_window_sum.11
  57.5 0.1 copy.28
  57.6 0.1 copy.27
  57.7 0.1 eq.64
  57.8 0.0 copy-start.3
  57.8 38.2 %collective-permute-done.1 = f32[64,7168]{1,0:T(8,128)} collective-permute-done((f32[64,7168]{1,0:T(8,128)}, f32[64,7168]{1,0:T(8,128)}, u32[]{:S(2)}, u32[]{:S(2)}) %collective-permute-start.1) | collective-permute-done | bytes 1835040 | tf_op jit(solution)/shard_map/ppermute | solution.py:37
  96.0 2.3 multiply_reduce_fusion
  98.4 0.0 copy-done.3
  98.4 3.0 convolution_convert_fusion.1
  101.5 7.0 %reshape.39 = bf16[64,4,7168]{2,1,0:T(4,128)(2,1)} reshape(bf16[256,7168]{1,0:T(8,128)(2,1)} %convolution_convert_fusion.1) | data formatting | bytes 7340032 | tf_op jit(solution)/shard_map/reshape | solution.py:48
  108.5 98.5 %all_to_all.10 = bf16[64,4,7168]{2,1,0:T(4,128)(2,1)} all-to-all(bf16[64,4,7168]{2,1,0:T(4,128)(2,1)} %reshape.39), channel_id=1, replica_groups=mesh['dp'=64,'tp'=4] {'dp'}, dimensions={0} | all-to-all | bytes 7340032 | tf_op jit(solution)/shard_map/all_to_all | solution.py:47
  206.9 6.7 %reshape.40 = bf16[256,7168]{1,0:T(8,128)(2,1)} reshape(bf16[64,4,7168]{2,1,0:T(4,128)(2,1)} %all_to_all.10) | data formatting | bytes 7340032 | tf_op jit(solution)/shard_map/reshape | solution.py:54
  213.7 4.4 %fusion.3 = f32[256,256]{1,0:T(8,128)S(1)} fusion(bf16[256,7168]{1,0:T(8,128)(2,1)} %reshape.40, bf16[1,7168,256]{2,1,0:T(8,128)(2,1)} %param.13), kind=kOutput, calls=%fused_computation.5 | convolution fusion | flops 939524096 | bytes 7602176 | tf_op jit(solution)/shard_map/dot_general | solution.py:55
  218.1 0.0 copy-done.1
  218.1 0.9 copy-done.6
  219.0 1.7 abs_reduce_fusion.1
  220.7 0.3 copy-done
  221.0 2.9 convolution_convert_fusion
  223.9 0.0 reduce-scatter.2.cloned.1.call-update
  223.9 0.0 copy-start.5
  224.0 42.3 %reduce-scatter.2.cloned.1.call-done = bf16[256,1792]{1,0:T(8,128)(2,1)} async-done(((bf16[256,7168]{1,0:T(8,128)(2,1)}), bf16[256,1792]{1,0:T(8,128)(2,1)}) %reduce-scatter.2.cloned.1.call-update) | async-done | bytes 917520 | tf_op jit(solution)/shard_map/reduce_scatter | solution.py:62
  266.2 2.5 convert_element_type.57
  268.8 10.6 %all-to-all-start.1 = ((bf16[64,4,1792]{2,1,0:T(4,128)(2,1)}), bf16[64,4,1792]{2,1,0:T(4,128)(2,1)S(1)}, u32[]{:S(2)}, u32[]{:S(2)}) async-start(bf16[64,4,1792]{2,1,0:T(4,128)(2,1)} %convert_element_type.57), calls=%async_computation.2 | async-start | bytes 1835008 | tf_op jit(solution)/shard_map/all_to_all | solution.py:65
  279.4 0.1 copy.29
  279.5 0.2 select_reduce_fusion
  279.7 0.1 copy.30
  279.8 0.1 fusion.19
  279.9 0.4 abs_reduce_fusion
  280.2 0.1 multiply_reduce_fusion.1
  280.3 0.7 compare_select_fusion
  281.0 76.8 %all-reduce = (f32[64]{0:T(128)S(1)}, f32[64]{0:T(128)S(1)}) all-reduce(f32[64]{0:T(128)S(1)} %multiply_reduce_fusion.1, f32[64]{0:T(128)S(1)} %compare_select_fusion), channel_id=1, replica_groups=mesh['dp'=64,'tp'=4] {'dp','tp'}, use_global_device_ids=true, to_apply=%region_7.8 | all-reduce | flops 128 | bytes 1024 | tf_op jit(solution)/shard_map/pmax | solution.py:84
  357.8 0.6 dynamic_slice.18
  358.4 0.6 dynamic_slice.17
  359.0 0.0 all-to-all-done.1
  359.0 1.3 add_convert_fusion
  (10 shorter events, 0.1 us)
Async XLA Ops:
  7.2 259.1 %reduce-scatter.2.cloned.1.call-start = ((), (), s32[]{:S(2)}) async-start(), calls=%async_computation.3 | async-start | bytes 4587520 | tf_op jit(solution)/shard_map/reduce_scatter | solution.py:62
  7.2 2.8 copy-start.2
  11.1 46.0 %copy-start.4 = (s32[64,8]{0,1:T(8,128)S(1)}, s32[64,8]{0,1:T(8,128)}, u32[]{:S(2)}) copy-start(s32[64,8]{0,1:T(8,128)} %param.11) | copy-start | bytes 6148
  11.1 40.5 %collective-permute-start = (f32[64,7168]{1,0:T(8,128)S(1)}, f32[64,7168]{1,0:T(8,128)S(1)}, u32[]{:S(2)}, u32[]{:S(2)}) collective-permute-start(f32[64,7168]{1,0:T(8,128)S(1)} %fusion.12), channel_id=1, source_target_pairs={{0,1},{1,0},{2,3},{3,2},{4,5},{5,4},{6,7},{7,6},{8,9},{9,8},{10,11... | collective-permute-start | bytes 5505032 | tf_op jit(solution)/shard_map/ppermute | solution.py:37
  53.1 42.9 %collective-permute-start.1 = (f32[64,7168]{1,0:T(8,128)}, f32[64,7168]{1,0:T(8,128)}, u32[]{:S(2)}, u32[]{:S(2)}) collective-permute-start(f32[64,7168]{1,0:T(8,128)} %add.40), channel_id=1, source_target_pairs={{0,2},{1,3},{2,0},{3,1},{4,6},{5,7},{6,4},{7,5},{8,10},{9,11},{10,... | collective-permute-start | bytes 5505032 | tf_op jit(solution)/shard_map/ppermute | solution.py:37
  57.8 40.6 %copy-start.3 = (f32[7168]{0:T(1024)S(1)}, f32[7168]{0:T(1024)}, u32[]{:S(2)}) copy-start(f32[7168]{0:T(1024)} %param.10) | copy-start | bytes 86020
  213.7 4.4 %copy-start.1 = (bf16[256,7168]{1,0:T(8,128)(2,1)S(1)}, bf16[256,7168]{1,0:T(8,128)(2,1)}, u32[]{:S(2)}) copy-start(bf16[256,7168]{1,0:T(8,128)(2,1)} %reshape.40) | copy-start | bytes 11010052
  213.7 5.3 %copy-start.6 = (bf16[1,7168,256]{2,1,0:T(8,128)(2,1)S(1)}, bf16[1,7168,256]{2,1,0:T(8,128)(2,1)}, u32[]{:S(2)}) copy-start(bf16[1,7168,256]{2,1,0:T(8,128)(2,1)} %param.14) | copy-start | bytes 11010052
  219.0 2.0 copy-start
  223.9 55.5 %copy-start.5 = (bf16[64,8]{0,1:T(8,128)(2,1)S(1)}, bf16[64,8]{0,1:T(8,128)(2,1)}, u32[]{:S(2)}) copy-start(bf16[64,8]{0,1:T(8,128)(2,1)} %param.12) | copy-start | bytes 3076
  268.8 90.2 %all-to-all-start.1 = ((bf16[64,4,1792]{2,1,0:T(4,128)(2,1)}), bf16[64,4,1792]{2,1,0:T(4,128)(2,1)S(1)}, u32[]{:S(2)}, u32[]{:S(2)}) async-start(bf16[64,4,1792]{2,1,0:T(4,128)(2,1)} %convert_element_type.57), calls=%async_computation.2 | async-start | bytes 1835008 | tf_op jit(solution)/shard_map/all_to_all | solution.py:65
Sparse Core Ops, SparseCore 0:
  224.1 42.1 reduce-scatter.1
